TPU v7x, 128 devices: a whole 4x4x4 slice. The times are simulated.
128 devices in a mesh: group: 8 (over y, core), within: 16 (over z, x).
Axes of the slice: x: 4, y: 4, z: 4, core: 2. Of those that a mesh axis runs over, the one named last changes fastest.
Arguments:
- tokens: bfloat16 [16384, 2048], P(('group', 'within')), may hold values from -6 to 6
- languages: int32 [16384], P(('group', 'within')), may hold values from 0 to 99, as said below
- lang_group: int32 [100], replicated, may hold values from 0 to 7, as said below
- group_gain: float32 [8, 2048], replicated, may hold values from 0.25 to 1.75
- group_w1: bfloat16 [8, 2048, 8192], P('group', None, 'within'), may hold values from -0.125 to 0.125
- group_b1: float32 [8, 8192], P('group', 'within'), may hold values from -3 to 3
- group_w2: bfloat16 [8, 8192, 2048], P('group', 'within'), may hold values from -0.0625 to 0.0625
- group_b2: float32 [8, 2048], replicated, may hold values from -3 to 3
- shared_gain: float32 [2048], replicated, may hold values from 0.25 to 1.75
- shared_w1: bfloat16 [2048, 8192], P(None, 'group'), may hold values from -0.125 to 0.125
- shared_b1: float32 [8192], P('group'), may hold values from -3 to 3
- shared_w2: bfloat16 [8192, 2048], P('group'), may hold values from -0.0625 to 0.0625
- shared_b2: float32 [2048], replicated, may hold values from -3 to 3
Outputs:
- encoded: bfloat16 [16384, 2048], P(('group', 'within'))
Inputs may be any that keep to these rules, and one draw needn't show every extreme that they name: `lang_group`: every language lies in one group and every group holds at least one language. Among the 128 tokens of one device (an aligned block), at most 24 have languages of one group, and in every block some group has exactly 24.
All inputs are finite; a program needn't handle non-finite values.
Results may differ from a plain program's by a relative error of at most 0.017.
Values may be sent and summed in bfloat16 or wider, within the bound.
No kernel may reach another device: no remote copies, remote signals or barrier semaphores. Data moves between devices by JAX's collectives and lax.ppermute only.
A program may use at most 128 MiB of HBM per device.

v0:
```python
import jax
import jax.numpy as jnp
from jax import lax
from jax.sharding import PartitionSpec as P


def layer_norm(values, gains):
    centre = jnp.mean(values, axis=-1, keepdims=True)
    centred = values - centre
    spread = jnp.mean(centred * centred, axis=-1, keepdims=True)
    return centred * lax.rsqrt(spread + 1e-05) * gains


def on_device(
    tokens,
    languages,
    lang_group,
    group_gain,
    group_w1,
    group_b1,
    group_w2,
    group_b2,
    shared_gain,
    shared_w1,
    shared_b1,
    shared_w2,
    shared_b2,
):
    tok_dev = tokens.shape[0]
    width_model = tokens.shape[1]
    num_groups = group_gain.shape[0]
    num_langs = lang_group.shape[0]
    capacity = 3 * tok_dev // (2 * lax.axis_size("group"))
    residual_in = tokens.astype(jnp.float32)
    lang_hit = (languages[:, None] == jnp.arange(num_langs, dtype=jnp.int32)[None, :]).astype(
        jnp.int32
    )
    group_of = jnp.sum(lang_hit * lang_group[None, :], axis=1)
    onehot = (group_of[:, None] == jnp.arange(num_groups, dtype=jnp.int32)[None, :]).astype(
        jnp.int32
    )
    earlier = jnp.cumsum(onehot, axis=0) - onehot
    slot_index = jnp.sum(earlier * onehot, axis=1)
    position = group_of * capacity + slot_index
    dispatch_map = (
        position[None, :] == jnp.arange(num_groups * capacity, dtype=jnp.int32)[:, None]
    ).astype(jnp.bfloat16)
    onehot_float = onehot.astype(jnp.float32)
    row_gains = jnp.dot(onehot_float, group_gain, precision=lax.Precision.HIGHEST)
    normed = layer_norm(residual_in, row_gains).astype(jnp.bfloat16)
    outgoing = jnp.dot(dispatch_map, normed, preferred_element_type=jnp.float32).astype(
        jnp.bfloat16
    )
    outgoing = outgoing.reshape(num_groups, capacity, width_model)
    arrived = lax.all_to_all(outgoing, "group", split_axis=0, concat_axis=0, tiled=True)
    group_rows = arrived.reshape(num_groups * capacity, width_model)
    first_proj = group_w1[0]
    first_bias = group_b1[0]
    second_proj = group_w2[0]
    hidden = jax.nn.relu(
        jnp.dot(
            lax.all_gather(group_rows, "within", axis=0, tiled=True),
            first_proj,
            preferred_element_type=jnp.float32,
        )
        + first_bias
    ).astype(jnp.bfloat16)
    selected = hidden
    summed = lax.psum_scatter(
        jnp.dot(selected, second_proj, preferred_element_type=jnp.float32).astype(jnp.bfloat16),
        "within",
        scatter_dimension=0,
        tiled=True,
    )
    returned = lax.all_to_all(
        summed.reshape(num_groups, capacity, width_model),
        "group",
        split_axis=0,
        concat_axis=0,
        tiled=True,
    )
    returned = returned.reshape(num_groups * capacity, width_model)
    group_out = lax.dot_general(
        dispatch_map, returned, (((0,), (0,)), ((), ())), preferred_element_type=jnp.float32
    )
    group_bias = jnp.dot(onehot_float, group_b2, precision=lax.Precision.HIGHEST)
    middle = residual_in + group_out + group_bias
    shared_in = layer_norm(middle, shared_gain).astype(jnp.bfloat16)
    shared_hidden = jax.nn.relu(
        jnp.dot(
            lax.all_gather(shared_in, "group", axis=0, tiled=True),
            shared_w1,
            preferred_element_type=jnp.float32,
        )
        + shared_b1
    ).astype(jnp.bfloat16)
    selected = shared_hidden
    shared_out = lax.psum_scatter(
        jnp.dot(selected, shared_w2, preferred_element_type=jnp.float32).astype(jnp.bfloat16),
        "group",
        scatter_dimension=0,
        tiled=True,
    ).astype(jnp.float32)
    return (middle + shared_out + shared_b2).astype(jnp.bfloat16)


def solution(mesh):
    placed = (
        P(("group", "within"), None),
        P(("group", "within")),
        P(),
        P(),
        P("group", None, "within"),
        P("group", "within"),
        P("group", "within", None),
        P(),
        P(),
        P(None, "group"),
        P("group"),
        P("group", None),
        P(),
    )
    return jax.shard_map(
        on_device,
        mesh=mesh,
        in_specs=placed,
        out_specs=P(("group", "within"), None),
        check_vma=False,
    )
```

profile of v0, /device:TPU:0, one launch (start us, length us, event | category | flops | bytes accessed | tf_op | source)
XLA Modules:
  0.0 346.0 jit_solution(16796450870467543149)
XLA Ops:
  6.5 1.3 convert_reduce_fusion
  7.9 1.3 fusion.10
  9.2 0.8 select_reduce_fusion
  10.0 0.1 fusion.17
  10.1 0.2 reduce_window_sum.11
  10.3 0.2 fusion.16
  10.5 2.2 fusion
  12.6 0.4 convolution_convert_fusion.2
  13.0 17.7 %all_to_all.10 = bf16[8,24,2048]{2,1,0:T(8,128)(2,1)} all-to-all(bf16[8,24,2048]{2,1,0:T(8,128)(2,1)S(1)} %bitcast.22), channel_id=1, replica_groups=mesh['group'=8,'within'=16] {'group'}, dimensions={0} | all-to-all | bytes 1572864 | tf_op jit(solution)/shard_map/all_to_all | solution.py:55
  30.7 0.0 reduce-scatter.3.cloned.1.call-start
  30.8 90.6 %all-gather.3.cloned.1.call-done = bf16[3072,2048]{1,0:T(8,128)(2,1)} async-done(((bf16[192,2048]{1,0:T(8,128)(2,1)}), bf16[3072,2048]{1,0:T(8,128)(2,1)}) %all-gather.3.cloned.1.call-update) | async-done | bytes 12582928 | tf_op jit(solution)/shard_map/all_gather | solution.py:62
  121.4 19.5 %convolution_convert_fusion = bf16[3072,2048]{1,0:T(8,128)(2,1)} fusion(bf16[1,512,2048]{2,1,0:T(8,128)(2,1)S(1)} %copy-done, bf16[3072,2048]{1,0:T(8,128)(2,1)} %all-gather.3.cloned.1.call-done, f32[512]{0:T(512)S(1)} %bitcast.24, bf16[1,2048,512]{2,1,0:T(8,128)(2,1)} %param.17), kind=kOutput, calls=%fused_computation | convolution fusion | flops 12895911936 | bytes 29362176 | tf_op jit(solution)/shard_map/dot_general | solution.py:70
  140.9 0.0 all-gather.5.cloned.1.call-start
  140.9 94.3 %reduce-scatter.3.cloned.1.call-done = bf16[192,2048]{1,0:T(8,128)(2,1)} async-done(((bf16[3072,2048]{1,0:T(8,128)(2,1)}), bf16[192,2048]{1,0:T(8,128)(2,1)}) %reduce-scatter.3.cloned.1.call-update) | async-done | bytes 786448 | tf_op jit(solution)/shard_map/reduce_scatter | solution.py:69
  235.2 17.5 %all_to_all.11 = bf16[8,24,2048]{2,1,0:T(8,128)(2,1)S(1)} all-to-all(bf16[8,24,2048]{2,1,0:T(8,128)(2,1)} %bitcast.23), channel_id=1, replica_groups=mesh['group'=8,'within'=16] {'group'}, dimensions={0} | all-to-all | bytes 1572864 | tf_op jit(solution)/shard_map/all_to_all | solution.py:75
  252.7 0.4 convolution_add_fusion.1
  253.1 1.1 fusion.24
  254.3 0.3 multiply_reduce_fusion
  254.5 1.0 multiply_convert_fusion
  255.6 0.2 reduce-scatter.5.cloned.1.call-start
  255.8 29.2 %all-gather.5.cloned.1.call-done = bf16[1024,2048]{1,0:T(8,128)(2,1)} async-done(((bf16[128,2048]{1,0:T(8,128)(2,1)}), bf16[1024,2048]{1,0:T(8,128)(2,1)}) %all-gather.5.cloned.1.call-update) | async-done | bytes 4194320 | tf_op jit(solution)/shard_map/all_gather | solution.py:91
  285.0 14.3 %convolution_convert_fusion.1 = bf16[1024,2048]{1,0:T(8,128)(2,1)} fusion(bf16[1024,2048]{1,0:T(8,128)(2,1)} %param.24, f32[1024]{0:T(1024)S(1)} %copy-done.5, bf16[1024,2048]{1,0:T(8,128)(2,1)} %all-gather.5.cloned.1.call-done, bf16[2048,1024]{1,0:T(8,128)(2,1)} %param.22), kind=kOutput, calls=%fused_computation.3 | convolution fusion | flops 8595177472 | bytes 16781312 | tf_op jit(solution)/shard_map/dot_general | solution.py:99
  299.4 38.1 %reduce-scatter.5.cloned.1.call-done = bf16[128,2048]{1,0:T(8,128)(2,1)} async-done(((bf16[1024,2048]{1,0:T(8,128)(2,1)}), bf16[128,2048]{1,0:T(8,128)(2,1)}) %reduce-scatter.5.cloned.1.call-update) | async-done | bytes 524304 | tf_op jit(solution)/shard_map/reduce_scatter | solution.py:98
  337.5 2.0 add_convert_fusion
  (24 shorter events, 0.1 us)
Async XLA Ops:
  6.5 114.8 %copy-start = (bf16[1,512,2048]{2,1,0:T(8,128)(2,1)S(1)}, bf16[1,512,2048]{2,1,0:T(8,128)(2,1)}, u32[]{:S(2)}) copy-start(bf16[1,512,2048]{2,1,0:T(8,128)(2,1)} %param.19) | copy-start | bytes 6291460
  6.5 114.8 %copy-start.6 = (f32[1,512]{1,0:T(1,128)S(1)}, f32[1,512]{1,0:T(1,128)}, u32[]{:S(2)}) copy-start(f32[1,512]{1,0:T(1,128)} %param.18) | copy-start | bytes 6148
  6.5 114.8 %all-gather.3.cloned.1.call-start = ((), (), s32[]{:S(2)}) async-start(), calls=%async_computation.4 | async-start | bytes 13369344 | tf_op jit(solution)/shard_map/all_gather | solution.py:62
  30.7 204.5 %reduce-scatter.3.cloned.1.call-start = ((), (), s32[]{:S(2)}) async-start(), calls=%async_computation.5 | async-start | bytes 13369344 | tf_op jit(solution)/shard_map/reduce_scatter | solution.py:69
  140.8 111.9 %copy-start.1 = (bf16[128,2048]{1,0:T(8,128)(2,1)S(1)}, bf16[128,2048]{1,0:T(8,128)(2,1)}, u32[]{:S(2)}) copy-start(bf16[128,2048]{1,0:T(8,128)(2,1)} %param.13) | copy-start | bytes 1572868
  140.8 112.3 %copy-start.2 = (f32[8,2048]{1,0:T(8,128)S(1)}, f32[8,2048]{1,0:T(8,128)}, u32[]{:S(2)}) copy-start(f32[8,2048]{1,0:T(8,128)} %param.20) | copy-start | bytes 196612
  140.9 113.7 %copy-start.3 = (f32[2048]{0:T(1024)S(1)}, f32[2048]{0:T(1024)}, u32[]{:S(2)}) copy-start(f32[2048]{0:T(1024)} %param.21) | copy-start | bytes 24580
  140.9 144.1 %all-gather.5.cloned.1.call-start = ((), (), s32[]{:S(2)}) async-start(), calls=%async_computation.6 | async-start | bytes 4718592 | tf_op jit(solution)/shard_map/all_gather | solution.py:91
  252.7 32.3 %copy-start.5 = (f32[1024]{0:T(1024)S(1)}, f32[1024]{0:T(1024)}, u32[]{:S(2)}) copy-start(f32[1024]{0:T(1024)} %param.23) | copy-start | bytes 12292
  255.6 81.9 %reduce-scatter.5.cloned.1.call-start = ((), (), s32[]{:S(2)}) async-start(), calls=%async_computation.7 | async-start | bytes 4718592 | tf_op jit(solution)/shard_map/reduce_scatter | solution.py:98
  299.3 38.1 %copy-start.4 = (f32[2048]{0:T(1024)S(1)}, f32[2048]{0:T(1024)}, u32[]{:S(2)}) copy-start(f32[2048]{0:T(1024)} %param.25) | copy-start | bytes 24580
Sparse Core Ops, SparseCore 0:
  30.8 90.4 all-gather.2
  141.0 94.1 reduce-scatter.2
  255.7 29.2 all-gather.4
  299.5 37.9 reduce-scatter.4
where the time goes:
time: 346 us
  waiting for transfers between devices  252 us (73%)
  matrix products  37.8 us (11%)
  blocking collectives  35.2 us (10%)
  between operations  13.2 us (4%)
  other arithmetic  7.17 us (2%)
    reduce_scatter x1, waiting for transfers between devices, on_device(): lax.psum_scatter(jnp.dot(selected, second_proj, preferred_element_type=jn...  94.3 us
    all_gather x1, waiting for transfers between devices, on_device(): lax.all_gather(group_rows, 'within', axis=0, tiled=True)  90.6 us
    reduce_scatter x1, waiting for transfers between devices, on_device(): lax.psum_scatter(jnp.dot(selected, shared_w2, preferred_element_type=jnp....  38.1 us
    all_gather x1, waiting for transfers between devices, on_device(): lax.all_gather(shared_in, 'group', axis=0, tiled=True)  29.2 us
    dot_general x1, matrix products, on_device(): jnp.dot(selected, second_proj, preferred_element_type=jnp.float32)  19.5 us
    all_to_all x1, blocking collectives, on_device(): lax.all_to_all(outgoing, 'group', split_axis=0, concat_axis=0, tiled=True)  17.7 us
    all_to_all x1, blocking collectives, on_device(): lax.all_to_all(summed.reshape(num_groups, capacity, width_model), 'group'...  17.5 us
    dot_general x1, matrix products, on_device(): jnp.dot(selected, shared_w2, preferred_element_type=jnp.float32)  14.3 us
  transfers between devices with their start and end apart: 4, of which 4 were waited for; matrix products, arithmetic and copies ran while one was open for 0% of the time, Pallas kernels for 0%

commit v1 on v0

--- a/solution.py
+++ b/solution.py
@@ -2,6 +2,13 @@
 import jax.numpy as jnp
 from jax import lax
 from jax.sharding import PartitionSpec as P
+
+
+def exchange_gather(x, name, dim):
+    peers = lax.axis_size(name)
+    blocks = jnp.stack([x for _ in range(peers)])
+    blocks = lax.all_to_all(blocks, name, split_axis=0, concat_axis=0)
+    return jnp.concatenate(blocks, axis=dim)
 
 
 def layer_norm(values, gains):
@@ -59,9 +66,7 @@
     second_proj = group_w2[0]
     hidden = jax.nn.relu(
         jnp.dot(
-            lax.all_gather(group_rows, "within", axis=0, tiled=True),
-            first_proj,
-            preferred_element_type=jnp.float32,
+            exchange_gather(group_rows, "within", 0), first_proj, preferred_element_type=jnp.float32
         )
         + first_bias
     ).astype(jnp.bfloat16)

time: 346 us -> 406 us (1.17)
  blocking collectives: 35.2 us -> 184 us
  waiting for transfers between devices: 252 us -> 158 us
  local copies, waits for them, and re-layouts: 0.03 us -> 6.13 us
    all_to_all x0 -> x1, blocking collectives: none -> 148 us  [exchange_gather(): blocks = lax.all_to_all(blocks, name, split_axis=0, concat_axis=0)]
    all_gather x1 -> x0, waiting for transfers between devices: 90.6 us -> none  [on_device(): lax.all_gather(group_rows, 'within', axis=0, tiled=True)]
    another operation x0 -> x1, local copies, waits for them, and re-layouts: none -> 6.11 us  [exchange_gather(): blocks = jnp.stack([x for _ in range(peers)])]
  transfers between devices with their start and end apart: 4 -> 3, of which waited for: 4 -> 3; matrix products, arithmetic and copies ran while one was open for 0% -> 0% of each run, Pallas kernels for 0% -> 0%
where the time goes in v1:
time: 406 us
  blocking collectives  184 us (45%)
  waiting for transfers between devices  158 us (39%)
  matrix products  37.8 us (9%)
  between operations  13.2 us (3%)
  other arithmetic  7.17 us (2%)
  local copies, waits for them, and re-layouts  6.13 us (2%)
    all_to_all x1, blocking collectives, exchange_gather(): blocks = lax.all_to_all(blocks, name, split_axis=0, concat_axis=0)  148 us
    reduce_scatter x1, waiting for transfers between devices, on_device(): lax.psum_scatter(jnp.dot(selected, second_proj, preferred_element_type=jn...  90.2 us
    reduce_scatter x1, waiting for transfers between devices, on_device(): lax.psum_scatter(jnp.dot(selected, shared_w2, preferred_element_type=jnp....  38.1 us
    all_gather x1, waiting for transfers between devices, on_device(): lax.all_gather(shared_in, 'group', axis=0, tiled=True)  29.2 us
    dot_general x1, matrix products, on_device(): jnp.dot(selected, second_proj, preferred_element_type=jnp.float32)  19.5 us
    all_to_all x1, blocking collectives, on_device(): lax.all_to_all(outgoing, 'group', split_axis=0, concat_axis=0, tiled=True)  17.6 us
    all_to_all x1, blocking collectives, on_device(): lax.all_to_all(summed.reshape(num_groups, capacity, width_model), 'group'...  17.5 us
    dot_general x1, matrix products, on_device(): jnp.dot(selected, shared_w2, preferred_element_type=jnp.float32)  14.3 us
  transfers between devices with their start and end apart: 3, of which 3 were waited for; matrix products, arithmetic and copies ran while one was open for 0% of the time, Pallas kernels for 0%

profile of v1, /device:TPU:0, one launch (start us, length us, event | category | flops | bytes accessed | tf_op | source)
XLA Modules:
  0.0 405.7 jit_solution(15099694195227286851)
XLA Ops:
  6.5 1.3 convert_reduce_fusion
  7.9 1.3 fusion.10
  9.2 0.8 select_reduce_fusion
  10.0 0.1 fusion.17
  10.1 0.2 reduce_window_sum.11
  10.3 0.2 fusion.16
  10.5 2.2 fusion
  12.6 0.4 convolution_convert_fusion.2
  13.0 17.6 %all_to_all.15 = bf16[8,24,2048]{2,1,0:T(8,128)(2,1)S(1)} all-to-all(bf16[8,24,2048]{2,1,0:T(8,128)(2,1)S(1)} %bitcast.24), channel_id=1, replica_groups=mesh['group'=8,'within'=16] {'group'}, dimensions={0} | all-to-all | bytes 1572864 | tf_op jit(solution)/shard_map/all_to_all | solution.py:62
  30.6 6.1 %stack.3 = bf16[16,192,2048]{2,1,0:T(8,128)(2,1)} broadcast(bf16[192,2048]{1,0:T(8,128)(2,1)S(1)} %bitcast.23), dimensions={1,2} | broadcast | bytes 13369344 | tf_op jit(solution)/shard_map/stack | solution.py:9
  36.7 148.5 %all_to_all.16 = bf16[16,192,2048]{2,1,0:T(8,128)(2,1)} all-to-all(bf16[16,192,2048]{2,1,0:T(8,128)(2,1)} %stack.3), channel_id=1, replica_groups=mesh['group'=8,'within'=16] {'within'}, dimensions={0} | all-to-all | bytes 25165824 | tf_op jit(solution)/shard_map/all_to_all | solution.py:10
  185.2 19.5 %convolution_convert_fusion = bf16[3072,2048]{1,0:T(8,128)(2,1)} fusion(bf16[1,512,2048]{2,1,0:T(8,128)(2,1)S(1)} %copy-done, bf16[3072,2048]{1,0:T(8,128)(2,1)} %bitcast.21, f32[512]{0:T(512)S(1)} %bitcast.26, bf16[1,2048,512]{2,1,0:T(8,128)(2,1)} %param.17), kind=kOutput, calls=%fused_computation | convolution fusion | flops 12895911936 | bytes 29362176 | tf_op jit(solution)/shard_map/dot_general | solution.py:75
  204.7 0.0 all-gather.2.cloned.1.call-start
  204.7 90.2 %reduce-scatter.3.cloned.1.call-done = bf16[192,2048]{1,0:T(8,128)(2,1)} async-done(((bf16[3072,2048]{1,0:T(8,128)(2,1)}), bf16[192,2048]{1,0:T(8,128)(2,1)}) %reduce-scatter.3.cloned.1.call-update) | async-done | bytes 786448 | tf_op jit(solution)/shard_map/reduce_scatter | solution.py:74
  294.9 17.5 %all_to_all.17 = bf16[8,24,2048]{2,1,0:T(8,128)(2,1)S(1)} all-to-all(bf16[8,24,2048]{2,1,0:T(8,128)(2,1)} %bitcast.25), channel_id=1, replica_groups=mesh['group'=8,'within'=16] {'group'}, dimensions={0} | all-to-all | bytes 1572864 | tf_op jit(solution)/shard_map/all_to_all | solution.py:80
  312.5 0.4 convolution_add_fusion.1
  312.8 1.1 fusion.24
  314.0 0.3 multiply_reduce_fusion
  314.3 1.0 multiply_convert_fusion
  315.3 0.2 reduce-scatter.5.cloned.1.call-start
  315.5 29.2 %all-gather.2.cloned.1.call-done = bf16[1024,2048]{1,0:T(8,128)(2,1)} async-done(((bf16[128,2048]{1,0:T(8,128)(2,1)}), bf16[1024,2048]{1,0:T(8,128)(2,1)}) %all-gather.2.cloned.1.call-update) | async-done | bytes 4194320 | tf_op jit(solution)/shard_map/all_gather | solution.py:96
  344.7 14.3 %convolution_convert_fusion.1 = bf16[1024,2048]{1,0:T(8,128)(2,1)} fusion(bf16[1024,2048]{1,0:T(8,128)(2,1)} %param.24, f32[1024]{0:T(1024)S(1)} %copy-done.5, bf16[1024,2048]{1,0:T(8,128)(2,1)} %all-gather.2.cloned.1.call-done, bf16[2048,1024]{1,0:T(8,128)(2,1)} %param.22), kind=kOutput, calls=%fused_computation.3 | convolution fusion | flops 8595177472 | bytes 16781312 | tf_op jit(solution)/shard_map/dot_general | solution.py:104
  359.1 38.1 %reduce-scatter.5.cloned.1.call-done = bf16[128,2048]{1,0:T(8,128)(2,1)} async-done(((bf16[1024,2048]{1,0:T(8,128)(2,1)}), bf16[128,2048]{1,0:T(8,128)(2,1)}) %reduce-scatter.5.cloned.1.call-update) | async-done | bytes 524304 | tf_op jit(solution)/shard_map/reduce_scatter | solution.py:103
  397.2 2.0 add_convert_fusion
  (23 shorter events, 0.1 us)
Async XLA Ops:
  6.5 178.7 %copy-start = (bf16[1,512,2048]{2,1,0:T(8,128)(2,1)S(1)}, bf16[1,512,2048]{2,1,0:T(8,128)(2,1)}, u32[]{:S(2)}) copy-start(bf16[1,512,2048]{2,1,0:T(8,128)(2,1)} %param.19) | copy-start | bytes 6291460
  6.5 288.4 %reduce-scatter.3.cloned.1.call-start = ((), (), s32[]{:S(2)}) async-start(), calls=%async_computation.5 | async-start | bytes 13369344 | tf_op jit(solution)/shard_map/reduce_scatter | solution.py:74
  36.7 148.5 %copy-start.6 = (f32[1,512]{1,0:T(1,128)S(1)}, f32[1,512]{1,0:T(1,128)}, u32[]{:S(2)}) copy-start(f32[1,512]{1,0:T(1,128)} %param.18) | copy-start | bytes 6148
  204.6 107.8 %copy-start.1 = (bf16[128,2048]{1,0:T(8,128)(2,1)S(1)}, bf16[128,2048]{1,0:T(8,128)(2,1)}, u32[]{:S(2)}) copy-start(bf16[128,2048]{1,0:T(8,128)(2,1)} %param.13) | copy-start | bytes 1572868
  204.7 108.2 %copy-start.2 = (f32[8,2048]{1,0:T(8,128)S(1)}, f32[8,2048]{1,0:T(8,128)}, u32[]{:S(2)}) copy-start(f32[8,2048]{1,0:T(8,128)} %param.20) | copy-start | bytes 196612
  204.7 109.6 %copy-start.3 = (f32[2048]{0:T(1024)S(1)}, f32[2048]{0:T(1024)}, u32[]{:S(2)}) copy-start(f32[2048]{0:T(1024)} %param.21) | copy-start | bytes 24580
  204.7 140.1 %all-gather.2.cloned.1.call-start = ((), (), s32[]{:S(2)}) async-start(), calls=%async_computation.6 | async-start | bytes 4718592 | tf_op jit(solution)/shard_map/all_gather | solution.py:96
  312.5 32.3 %copy-start.5 = (f32[1024]{0:T(1024)S(1)}, f32[1024]{0:T(1024)}, u32[]{:S(2)}) copy-start(f32[1024]{0:T(1024)} %param.23) | copy-start | bytes 12292
  315.3 81.9 %reduce-scatter.5.cloned.1.call-start = ((), (), s32[]{:S(2)}) async-start(), calls=%async_computation.7 | async-start | bytes 4718592 | tf_op jit(solution)/shard_map/reduce_scatter | solution.py:103
  359.1 38.1 %copy-start.4 = (f32[2048]{0:T(1024)S(1)}, f32[2048]{0:T(1024)}, u32[]{:S(2)}) copy-start(f32[2048]{0:T(1024)} %param.25) | copy-start | bytes 24580
Sparse Core Ops, SparseCore 0:
  204.8 90.1 reduce-scatter.2
  315.4 29.2 all-gather.1
  359.2 37.9 reduce-scatter.4
